TPU v7x, 128 devices: a whole 4x4x4 slice. The times are simulated.
128 devices in a mesh: section: 4 (over y_lo, core), dp: 16 (over z, x), mp: 2 (over y_hi).
Axes of the slice: x: 4, y: 4 (y_hi: 2, y_lo: 2; y = y_hi * 2 + y_lo), z: 4, core: 2. Of those that a mesh axis runs over, the one named last changes fastest.
Arguments:
- siglip_features: bfloat16 [8192, 1152], P('dp'), may hold values from -6 to 6
- convnext_features: bfloat16 [8192, 1536], P('dp'), may hold values from -6 to 6
- siglip_projection: bfloat16 [1152, 8192], P(None, ('section', 'mp')), may hold values from -0.125 to 0.125
- convnext_projection: bfloat16 [1536, 8192], P(None, ('section', 'mp')), may hold values from -0.125 to 0.125
- newline_embed: bfloat16 [8192], P(('section', 'mp')), may hold values from -6 to 6
- key_value_weight: bfloat16 [2048, 8192], P(None, ('section', 'mp')), may hold values from -0.0625 to 0.0625
- tile_rank: int32 [256, 1], replicated, may hold values from 0 to 15; in each aligned block of 16 rows (0 to 15, 16 to 31, ...) at most 2 rows name the same one
- row_end: int32 [256], replicated, may hold values 0 or 1
- key_value_grad: bfloat16 [16384, 2048], P('dp'), may hold values from -0.059814453 to 0.059814453
- newline_grad: bfloat16 [512, 2048], P('dp'), may hold values from -1.796875 to 1.796875
Outputs:
- siglip_weight_grad: float32 [1152, 8192], P('dp', ('section', 'mp'))
- convnext_weight_grad: float32 [1536, 8192], P('dp', ('section', 'mp'))
- key_value_weight_grad: float32 [2048, 8192], P('dp', ('section', 'mp'))
Inputs may be any that keep to these rules, and one draw needn't show every extreme that they name: `tile_rank`: each aligned block of 16 tiles (the tiles of one index of dp) sends at most 2 tiles to one rank, and exactly 2 to some rank.
All inputs are finite; a program needn't handle non-finite values.
Results may differ from a plain program's by a relative error of at most 0.007.
Values may be sent and summed in bfloat16 or wider, within the bound.
No kernel may reach another device: no remote copies, remote signals or barrier semaphores. Data moves between devices by JAX's collectives and lax.ppermute only.
A program may use at most 128 MiB of HBM per device.

v0:
```python
import jax
import jax.numpy as jnp
from jax import lax
from jax.sharding import PartitionSpec as P

D = 8192
epsilon = 1e-06


def tile_places(tile_rank, groups):
    dest_rank = tile_rank[:, 0]
    tile_count = dest_rank.shape[0]
    per_device = tile_count // groups
    onehot = (dest_rank[:, None] == jnp.arange(groups, dtype=jnp.int32)[None, :]).astype(jnp.int32)
    blocks = onehot.reshape(groups, per_device, groups)
    before = jnp.cumsum(blocks, axis=1) - blocks
    slot_place = jnp.sum(before * blocks, axis=2).reshape(tile_count)
    source = jnp.arange(tile_count, dtype=jnp.int32) // per_device
    return (dest_rank, source, slot_place)


def row_norms(squares):
    return lax.psum((squares[0], squares[1]), ("section", "mp"))


def row_products(products):
    return lax.psum(products, ("section", "mp"))


def norm_backward(inverse_rms, grad_values, proj_values):
    products = row_products(jnp.sum(grad_values * proj_values, axis=1))[:, None]
    return (inverse_rms * grad_values - inverse_rms**3 * proj_values * products / D).astype(
        jnp.bfloat16
    )


def local(
    siglip_features,
    convnext_features,
    siglip_projection,
    convnext_projection,
    newline_embed,
    key_value_weight,
    tile_rank,
    row_end,
    key_value_grad,
    newline_grad,
):
    groups = lax.axis_size("dp")
    my_rank = lax.axis_index("dp")
    dest_rank, source, slot_place = tile_places(tile_rank, groups)
    per_device = dest_rank.shape[0] // groups
    capacity = 2 * per_device // groups
    row_count = siglip_features.shape[0]
    tile_rows = row_count // per_device
    share = siglip_projection.shape[1]
    mine_dest = lax.dynamic_slice_in_dim(dest_rank, my_rank * per_device, per_device)
    mine_place = lax.dynamic_slice_in_dim(slot_place, my_rank * per_device, per_device)
    rank_ids = jnp.arange(groups, dtype=jnp.int32)[:, None, None]
    place_ids = jnp.arange(capacity, dtype=jnp.int32)[None, :, None]
    select = (
        (mine_dest[None, None, :] == rank_ids) & (mine_place[None, None, :] == place_ids)
    ).astype(jnp.bfloat16)
    projected = (
        jnp.dot(siglip_features, siglip_projection, preferred_element_type=jnp.float32)
        + jnp.dot(convnext_features, convnext_projection, preferred_element_type=jnp.float32)
    ).astype(jnp.bfloat16)
    line_vector = newline_embed.astype(jnp.float32)
    line_square = jnp.sum(line_vector * line_vector)
    outgoing = jnp.einsum(
        "gcj,jtx->gctx",
        select,
        projected.reshape(per_device, tile_rows, share),
        preferred_element_type=jnp.float32,
    ).astype(jnp.bfloat16)
    outgoing = outgoing.reshape(groups, capacity * tile_rows, share)
    received = lax.all_to_all(outgoing, "dp", split_axis=0, concat_axis=0, tiled=True).reshape(
        groups * capacity * tile_rows, share
    )
    recv_values = received.astype(jnp.float32)
    statistic = row_norms((jnp.sum(recv_values * recv_values, axis=1), line_square))
    recv_inverse = lax.rsqrt(statistic[0] / D + epsilon)[:, None]
    line_total_sq = statistic[1]
    normed = (recv_values * recv_inverse).astype(jnp.bfloat16)
    line_normed = (line_vector * lax.rsqrt(line_total_sq / D + epsilon)).astype(jnp.bfloat16)
    slot_global = source * capacity + slot_place
    line_live = (dest_rank == my_rank) & (row_end == 1)
    slot_ids = jnp.arange(groups * capacity, dtype=jnp.int32)[None, :]
    newline_mask = jnp.sum(
        ((slot_global[:, None] == slot_ids) & line_live[:, None]).astype(jnp.int32), axis=0
    )
    line_total = jnp.dot(
        newline_mask.astype(jnp.bfloat16)[None, :], newline_grad, preferred_element_type=jnp.float32
    )[0]
    kv_term = lax.dot_general(
        key_value_grad, normed, (((0,), (0,)), ((), ())), preferred_element_type=jnp.float32
    )
    kv_term = kv_term + line_total[:, None] * line_normed.astype(jnp.float32)[None, :]
    normed_grad = jnp.dot(
        key_value_grad, key_value_weight, preferred_element_type=jnp.float32
    ).astype(jnp.bfloat16)
    returning = norm_backward(recv_inverse, normed_grad.astype(jnp.float32), recv_values)
    returned = lax.all_to_all(
        returning.reshape(groups, capacity * tile_rows, share),
        "dp",
        split_axis=0,
        concat_axis=0,
        tiled=True,
    )
    tile_back = jnp.einsum(
        "gcj,gctx->jtx",
        select,
        returned.reshape(groups, capacity, tile_rows, share),
        preferred_element_type=jnp.float32,
    ).reshape(row_count, share)
    projected_grad = tile_back.astype(jnp.bfloat16)
    contract = (((0,), (0,)), ((), ()))
    siglip_term = lax.dot_general(
        siglip_features, projected_grad, contract, preferred_element_type=jnp.float32
    )
    convnext_term = lax.dot_general(
        convnext_features, projected_grad, contract, preferred_element_type=jnp.float32
    )
    siglip_result, convnext_result, kv_result = (
        lax.psum_scatter(siglip_term, "dp", scatter_dimension=0, tiled=True),
        lax.psum_scatter(convnext_term, "dp", scatter_dimension=0, tiled=True),
        lax.psum_scatter(kv_term, "dp", scatter_dimension=0, tiled=True),
    )
    return (siglip_result, convnext_result, kv_result)


def solution(mesh):
    in_specs = (
        P("dp", None),
        P("dp", None),
        P(None, ("section", "mp")),
        P(None, ("section", "mp")),
        P(("section", "mp")),
        P(None, ("section", "mp")),
        P(),
        P(),
        P("dp", None),
        P("dp", None),
    )
    out_specs = (P("dp", ("section", "mp")), P("dp", ("section", "mp")), P("dp", ("section", "mp")))
    return jax.shard_map(local, mesh=mesh, in_specs=in_specs, out_specs=out_specs, check_vma=False)
```

profile of v0, /device:TPU:0, one launch (start us, length us, event | category | flops | bytes accessed | tf_op | source)
XLA Modules:
  0.0 415.1 jit_solution(3388433435332822408)
XLA Ops:
  7.2 0.0 copy-start
  7.2 0.5 broadcast.91
  7.7 1.6 reduce.6
  9.3 0.1 eq.84
  9.4 0.1 copy.51
  9.5 0.5 fusion.29
  9.9 0.1 copy.52
  10.0 0.1 reshape.120
  10.1 0.7 dynamic-slice_bitcast_fusion
  10.8 0.1 dynamic_slice.7
  10.9 0.1 iota_compare_fusion.3
  11.0 0.0 copy-start.8
  11.0 3.7 fusion.30
  14.6 0.0 copy-done
  14.7 0.0 copy-done.8
  14.7 1.8 add_convert_fusion
  16.5 1.0 convolution_convert_fusion.1
  17.4 2.5 copy.55
  19.9 0.0 copy-start.5
  19.9 8.1 %all-to-all-start = ((bf16[16,64,1024]{2,1,0:T(8,128)(2,1)}), bf16[16,64,1024]{2,1,0:T(8,128)(2,1)S(1)}, u32[]{:S(2)}, u32[]{:S(2)}) async-start(bf16[16,64,1024]{2,1,0:T(8,128)(2,1)} %copy.55), calls=%async_computation | async-start | bytes 4194304 | tf_op jit(solution)/shard_map/all_to_all | solution.py:77
  28.0 0.0 all-reduce.4.cloned.1.call-start
  28.1 0.0 copy-done.5
  28.1 0.6 fusion.21
  28.7 31.0 %all-to-all-done = bf16[16,64,1024]{2,1,0:T(8,128)(2,1)S(1)} async-done(((bf16[16,64,1024]{2,1,0:T(8,128)(2,1)}), bf16[16,64,1024]{2,1,0:T(8,128)(2,1)S(1)}, u32[]{:S(2)}, u32[]{:S(2)}) %all-to-all-start) | async-done | bytes 2097184 | tf_op jit(solution)/shard_map/all_to_all | solution.py:77
  59.7 0.5 fusion.3
  60.2 0.1 reduce_sum.49
  60.2 9.2 %fusion.2 = (f32[1024]{0:T(1024)S(1)}, bf16[1024,1024]{1,0:T(8,128)(2,1)}) fusion(bf16[16,64,1024]{2,1,0:T(8,128)(2,1)S(1)} %all-to-all-done, bf16[1024,2048]{1,0:T(8,128)(2,1)} %param.18, bf16[2048,1024]{1,0:T(8,128)(2,1)} %param.15), kind=kOutput, calls=%fused_computation.7 | convolution fusion | flops 4300209152 | bytes 12587008 | tf_op jit(solution)/shard_map/dot_general | solution.py:99
  69.5 18.3 %all-reduce.1 = (f32[1024]{0:T(1024)S(1)}, f32[1024]{0:T(1024)S(1)}, f32[]{:T(128)}) all-reduce(f32[1024]{0:T(1024)S(1)} %get-tuple-element.25, f32[1024]{0:T(1024)S(1)} %reduce_sum.49, f32[]{:T(128)} %fusion.21), channel_id=1, replica_groups=mesh['section'=4,'dp'=16,'mp'=2] {'section','mp'}, use_global_device_ids=true, to_apply=%region_5.6 | all-reduce | flops 2049 | bytes 16392 | tf_op jit(solution)/shard_map/psum | solution.py:27
  87.9 3.8 fusion.6
  91.6 32.7 %all_to_all.10 = bf16[16,64,1024]{2,1,0:T(8,128)(2,1)S(1)} all-to-all(bf16[16,64,1024]{2,1,0:T(8,128)(2,1)S(1)} %bitcast.61), channel_id=1, replica_groups=mesh['section'=4,'dp'=16,'mp'=2] {'dp'}, dimensions={0} | all-to-all | bytes 4194304 | tf_op jit(solution)/shard_map/all_to_all | solution.py:103
  124.3 0.0 copy-start.3
  124.3 2.4 bitcast_convert_fusion
  126.7 0.6 copy.59
  127.3 0.0 copy-done.3
  127.3 3.8 convolution_bitcast_fusion.1
  131.1 0.0 copy-start.6
  131.1 0.0 copy-start.7
  131.1 0.0 copy-start.4
  131.1 0.0 copy-start.2
  131.1 0.0 all-reduce.4.cloned.1.call-update
  131.1 0.0 reduce-scatter.6.cloned.1.call-start
  131.2 0.6 copy-done.6
  131.8 0.0 copy-done.7
  131.8 0.1 convert_reduce_fusion
  131.9 0.1 copy-done.4
  132.0 0.1 fusion.26
  132.9 0.0 copy-done.2
  132.9 9.7 %bitcast_add_fusion = f32[2048,1024]{0,1:T(8,128)} fusion(bf16[1024,1024]{1,0:T(8,128)(2,1)S(1)} %copy-done.2, bf16[1024,2048]{1,0:T(8,128)(2,1)} %param.18, f32[1024]{0:T(1024)S(1)} %fusion.23, f32[2048]{0:T(1024)S(1)} %bitcast.67), kind=kOutput, calls=%fused_computation | convolution fusion | flops 4299161600 | bytes 14692352 | tf_op jit(solution)/shard_map/dot_general | solution.py:95
  142.6 0.0 copy-start.9
  142.6 0.0 reduce-scatter.6.cloned.1.call-update
  142.6 0.0 reduce-scatter.8.cloned.1.call-start
  142.7 1.3 copy-done.9
  144.0 4.4 %convolution_bitcast_fusion = f32[1536,1024]{0,1:T(8,128)} fusion(bf16[512,1024]{1,0:T(8,128)(2,1)S(1)} %bitcast.65, bf16[512,1536]{1,0:T(8,128)(2,1)S(1)} %copy-done.9), kind=kOutput, calls=%fused_computation.3 | convolution fusion | flops 1610612736 | bytes 8912896 | tf_op jit(solution)/shard_map/dot_general | solution.py:121
  148.4 6.7 %copy.69 = f32[1536,1024]{1,0:T(8,128)} copy(f32[1536,1024]{0,1:T(8,128)} %convolution_bitcast_fusion) | data formatting | bytes 12582912
  155.1 0.0 reduce-scatter.8.cloned.1.call-update
  155.1 0.8 copy-done.10
  155.9 0.6 dynamic-slice.1
  157.2 77.5 %all-reduce.4.cloned.1.call-done = f32[1152,1024]{0,1:T(8,128)} async-done(((f32[1152,1024]{0,1:T(8,128)}), f32[1152,1024]{0,1:T(8,128)}) %all-reduce.4.cloned.1.call-update) | async-done | bytes 4718608
  234.6 2.2 constant_dynamic-slice_fusion
  236.8 1.9 copy.60
  238.8 84.4 %reduce-scatter.6.cloned.1.call-done = f32[128,1024]{0,1:T(8,128)} async-done(((f32[2048,1024]{0,1:T(8,128)}), f32[128,1024]{0,1:T(8,128)}) %reduce-scatter.6.cloned.1.call-update) | async-done | bytes 524304 | tf_op jit(solution)/shard_map/reduce_scatter | solution.py:127
  323.2 2.0 copy.62
  325.2 83.3 %reduce-scatter.8.cloned.1.call-done = f32[96,1024]{1,0:T(8,128)} async-done(((f32[1536,1024]{1,0:T(8,128)}), f32[96,1024]{1,0:T(8,128)}) %reduce-scatter.8.cloned.1.call-update) | async-done | bytes 393232
  408.5 0.0 copy-done.1
  (8 shorter events, 0.1 us)
Async XLA Ops:
  7.2 7.5 %copy-start = (bf16[1536,1024]{1,0:T(8,128)(2,1)S(1)}, bf16[1536,1024]{1,0:T(8,128)(2,1)}, u32[]{:S(2)}) copy-start(bf16[1536,1024]{1,0:T(8,128)(2,1)} %param.13) | copy-start | bytes 9437188
  11.0 3.7 copy-start.8
  19.9 8.2 %copy-start.5 = (bf16[1024]{0:T(1024)(128)(2,1)S(1)}, bf16[1024]{0:T(1024)(128)(2,1)}, u32[]{:S(2)}) copy-start(bf16[1024]{0:T(1024)(128)(2,1)} %param.14) | copy-start | bytes 6148
  19.9 39.8 %all-to-all-start = ((bf16[16,64,1024]{2,1,0:T(8,128)(2,1)}), bf16[16,64,1024]{2,1,0:T(8,128)(2,1)S(1)}, u32[]{:S(2)}, u32[]{:S(2)}) async-start(bf16[16,64,1024]{2,1,0:T(8,128)(2,1)} %copy.55), calls=%async_computation | async-start | bytes 4194304 | tf_op jit(solution)/shard_map/all_to_all | solution.py:77
  28.0 206.6 %all-reduce.4.cloned.1.call-start = ((), (), s32[]{:S(2)}) async-start(), calls=%async_computation.6 | async-start | bytes 9437184
  124.3 3.0 copy-start.3
  131.1 0.7 copy-start.6
  131.1 0.7 copy-start.7
  131.1 0.9 copy-start.4
  131.1 1.8 copy-start.2
  131.1 192.0 %reduce-scatter.6.cloned.1.call-start = ((), (), s32[]{:S(2)}) async-start(), calls=%async_computation.4 | async-start | bytes 8912896 | tf_op jit(solution)/shard_map/reduce_scatter | solution.py:127
  142.6 1.4 copy-start.9
  142.6 265.9 %reduce-scatter.8.cloned.1.call-start = ((), (), s32[]{:S(2)}) async-start(), calls=%async_computation.5 | async-start | bytes 6684672
  155.1 253.4 %copy-start.1 = (bf16[1536,1024]{1,0:T(8,128)(2,1)S(1)}, bf16[1536,1024]{1,0:T(8,128)(2,1)}, u32[]{:S(2)}) copy-start(bf16[1536,1024]{1,0:T(8,128)(2,1)} %param.13) | copy-start | bytes 9437188
  155.1 0.8 copy-start.10
Sparse Core Ops, SparseCore 0:
  131.3 103.2 all-reduce.3
  238.4 84.7 reduce-scatter.5
  327.6 80.9 reduce-scatter.7
where the time goes:
time: 416 us; the launch traced here: 415 us
  waiting for transfers between devices  276 us (66%)
  blocking collectives  51.1 us (12%)
  matrix products  36.1 us (9%)
  local copies, waits for them, and re-layouts  21.1 us (5%)
  between operations  15.2 us (4%)
  starting transfers between devices  8.22 us (2%)
  other arithmetic  7.15 us (2%)
    unnamed x5, waiting for transfers between devices  161 us
    reduce_scatter x1, waiting for transfers between devices, local(): lax.psum_scatter(kv_term, 'dp', scatter_dimension=0, tiled=True)  84.4 us
    all_to_all x1, blocking collectives, local(): lax.all_to_all(returning.reshape(groups, capacity * tile_rows, share), 'd...  32.7 us
    all_to_all x1, waiting for transfers between devices, local(): lax.all_to_all(outgoing, 'dp', split_axis=0, concat_axis=0, tiled=True)  31 us
    psum x1, blocking collectives, row_products(): return lax.psum(products, ('section', 'mp'))  18.3 us
    unnamed x28, local copies, waits for them, and re-layouts  16.9 us
    dot_general x1, matrix products, local(): lax.dot_general(key_value_grad, normed, (((0,), (0,)), ((), ())), preferr...  9.68 us
    dot_general x1, matrix products, local(): jnp.dot(key_value_grad, key_value_weight, preferred_element_type=jnp.floa...  9.25 us
  transfers between devices with their start and end apart: 4, of which 4 were waited for; matrix products, arithmetic and copies ran while one was open for 7% of the time, Pallas kernels for 0%

commit v1 on v0

--- a/solution.py
+++ b/solution.py
@@ -24,7 +24,7 @@
 
 
 def row_products(products):
-    return lax.psum(products, ("section", "mp"))
+    return jnp.sum(lax.all_gather(products, ("section", "mp")), axis=0)
 
 
 def norm_backward(inverse_rms, grad_values, proj_values):

time: 416 us -> 441 us (1.060)
  blocking collectives: 51.1 us -> 75.7 us
    all_gather x0 -> x1, blocking collectives: none -> 26 us  [row_products(): return jnp.sum(lax.all_gather(products, ('section', 'mp')), axis=0)]
  transfers between devices with their start and end apart: 4 -> 4, of which waited for: 4 -> 4; matrix products, arithmetic and copies ran while one was open for 7% -> 6% of each run, Pallas kernels for 0% -> 0%
where the time goes in v1:
time: 441 us; the launch traced here: 440 us
  waiting for transfers between devices  277 us (63%)
  blocking collectives  75.7 us (17%)
  matrix products  35.5 us (8%)
  local copies, waits for them, and re-layouts  21.1 us (5%)
  between operations  15.2 us (3%)
  starting transfers between devices  8.22 us (2%)
  other arithmetic  7.17 us (2%)
    unnamed x5, waiting for transfers between devices  162 us
    reduce_scatter x1, waiting for transfers between devices, local(): lax.psum_scatter(kv_term, 'dp', scatter_dimension=0, tiled=True)  84.4 us
    all_to_all x1, blocking collectives, local(): lax.all_to_all(returning.reshape(groups, capacity * tile_rows, share), 'd...  31.7 us
    all_to_all x1, waiting for transfers between devices, local(): lax.all_to_all(outgoing, 'dp', split_axis=0, concat_axis=0, tiled=True)  31 us
    all_gather x1, blocking collectives, row_products(): return jnp.sum(lax.all_gather(products, ('section', 'mp')), axis=0)  26 us
    psum x1, blocking collectives, row_norms(): return lax.psum((squares[0], squares[1]), ('section', 'mp'))  18 us
    unnamed x28, local copies, waits for them, and re-layouts  16.8 us
    dot_general x1, matrix products, local(): jnp.dot(key_value_grad, key_value_weight, preferred_element_type=jnp.floa...  9.25 us
  transfers between devices with their start and end apart: 4, of which 4 were waited for; matrix products, arithmetic and copies ran while one was open for 6% of the time, Pallas kernels for 0%

profile of v1, /device:TPU:0, one launch (start us, length us, event | category | flops | bytes accessed | tf_op | source)
XLA Modules:
  0.0 440.3 jit_solution(16360635901351776524)
XLA Ops:
  7.2 0.0 copy-start
  7.2 0.5 broadcast.91
  7.7 1.6 reduce.6
  9.3 0.1 eq.84
  9.4 0.1 copy.51
  9.5 0.5 fusion.29
  9.9 0.1 copy.52
  10.0 0.1 reshape.120
  10.1 0.7 dynamic-slice_bitcast_fusion
  10.8 0.1 dynamic_slice.7
  10.9 0.1 iota_compare_fusion.3
  11.0 0.0 copy-start.8
  11.0 3.7 fusion.30
  14.6 0.0 copy-done
  14.7 0.0 copy-done.8
  14.7 1.8 add_convert_fusion
  16.5 1.0 convolution_convert_fusion.1
  17.4 2.5 copy.55
  19.9 0.0 copy-start.5
  19.9 8.1 %all-to-all-start = ((bf16[16,64,1024]{2,1,0:T(8,128)(2,1)}), bf16[16,64,1024]{2,1,0:T(8,128)(2,1)S(1)}, u32[]{:S(2)}, u32[]{:S(2)}) async-start(bf16[16,64,1024]{2,1,0:T(8,128)(2,1)} %copy.55), calls=%async_computation | async-start | bytes 4194304 | tf_op jit(solution)/shard_map/all_to_all | solution.py:77
  28.0 0.0 all-reduce.4.cloned.1.call-start
  28.1 0.0 copy-done.5
  28.1 0.6 fusion.21
  28.7 31.0 %all-to-all-done = bf16[16,64,1024]{2,1,0:T(8,128)(2,1)S(1)} async-done(((bf16[16,64,1024]{2,1,0:T(8,128)(2,1)}), bf16[16,64,1024]{2,1,0:T(8,128)(2,1)S(1)}, u32[]{:S(2)}, u32[]{:S(2)}) %all-to-all-start) | async-done | bytes 2097184 | tf_op jit(solution)/shard_map/all_to_all | solution.py:77
  59.7 0.5 fusion.3
  60.2 0.1 reduce_sum.58
  60.2 18.0 %all-reduce.1 = (f32[1024]{0:T(1024)S(1)}, f32[]{:T(128)}) all-reduce(f32[1024]{0:T(1024)S(1)} %reduce_sum.58, f32[]{:T(128)} %fusion.21), channel_id=1, replica_groups=mesh['section'=4,'dp'=16,'mp'=2] {'section','mp'}, use_global_device_ids=true, to_apply=%region_3.4 | all-reduce | flops 1025 | bytes 8200 | tf_op jit(solution)/shard_map/psum | solution.py:23
  78.3 9.3 %fusion.2 = (f32[1024]{0:T(1024)S(1)}, bf16[1024,1024]{1,0:T(8,128)(2,1)}) fusion(bf16[16,64,1024]{2,1,0:T(8,128)(2,1)S(1)} %all-to-all-done, bf16[1024,2048]{1,0:T(8,128)(2,1)} %param.18, bf16[2048,1024]{1,0:T(8,128)(2,1)} %param.15), kind=kOutput, calls=%fused_computation.7 | convolution fusion | flops 4300209152 | bytes 12587008 | tf_op jit(solution)/shard_map/dot_general | solution.py:99
  87.6 26.0 %all-gather = f32[8192]{0:T(1024)S(1)} all-gather(f32[1024]{0:T(1024)S(1)} %get-tuple-element.24), channel_id=2, replica_groups=mesh['section'=4,'dp'=16,'mp'=2] {'section','mp'}, dimensions={0}, use_global_device_ids=true | all-gather | bytes 36864 | tf_op jit(solution)/shard_map/all_gather | solution.py:27
  113.6 3.8 fusion.6
  117.3 31.7 %all_to_all.10 = bf16[16,64,1024]{2,1,0:T(8,128)(2,1)S(1)} all-to-all(bf16[16,64,1024]{2,1,0:T(8,128)(2,1)S(1)} %bitcast.61), channel_id=1, replica_groups=mesh['section'=4,'dp'=16,'mp'=2] {'dp'}, dimensions={0} | all-to-all | bytes 4194304 | tf_op jit(solution)/shard_map/all_to_all | solution.py:103
  149.0 0.0 copy-start.3
  149.0 2.4 bitcast_convert_fusion
  151.4 0.6 copy.59
  152.0 0.0 copy-done.3
  152.0 3.8 convolution_bitcast_fusion.1
  155.8 0.0 copy-start.6
  155.8 0.0 copy-start.7
  155.8 0.0 copy-start.4
  155.8 0.0 all-reduce.4.cloned.1.call-update
  155.8 0.0 reduce-scatter.6.cloned.1.call-start
  155.9 0.6 copy-done.6
  156.5 0.0 copy-done.7
  156.5 0.1 convert_reduce_fusion
  156.7 0.1 copy-done.4
  156.7 0.1 fusion.26
  157.6 0.0 copy-done.2
  157.6 9.2 %bitcast_add_fusion = f32[2048,1024]{0,1:T(8,128)} fusion(bf16[1024,1024]{1,0:T(8,128)(2,1)S(1)} %copy-done.2, bf16[1024,2048]{1,0:T(8,128)(2,1)} %param.18, f32[1024]{0:T(1024)S(1)} %fusion.23, f32[2048]{0:T(1024)S(1)} %bitcast.67), kind=kOutput, calls=%fused_computation | convolution fusion | flops 4299161600 | bytes 14692352 | tf_op jit(solution)/shard_map/dot_general | solution.py:95
  166.8 0.0 reduce-scatter.6.cloned.1.call-update
  166.8 0.0 reduce-scatter.8.cloned.1.call-start
  166.8 1.4 copy-done.9
  168.2 4.4 convolution_bitcast_fusion
  172.6 6.7 %copy.69 = f32[1536,1024]{1,0:T(8,128)} copy(f32[1536,1024]{0,1:T(8,128)} %convolution_bitcast_fusion) | data formatting | bytes 12582912
  179.3 0.0 copy-start.1
  179.3 0.0 reduce-scatter.8.cloned.1.call-update
  179.3 0.8 copy-done.10
  180.1 0.6 dynamic-slice.1
  181.3 78.5 %all-reduce.4.cloned.1.call-done = f32[1152,1024]{0,1:T(8,128)} async-done(((f32[1152,1024]{0,1:T(8,128)}), f32[1152,1024]{0,1:T(8,128)}) %all-reduce.4.cloned.1.call-update) | async-done | bytes 4718608
  259.8 2.2 constant_dynamic-slice_fusion
  262.0 1.9 copy.60
  264.0 84.4 %reduce-scatter.6.cloned.1.call-done = f32[128,1024]{0,1:T(8,128)} async-done(((f32[2048,1024]{0,1:T(8,128)}), f32[128,1024]{0,1:T(8,128)}) %reduce-scatter.6.cloned.1.call-update) | async-done | bytes 524304 | tf_op jit(solution)/shard_map/reduce_scatter | solution.py:127
  348.4 2.0 copy.62
  350.4 83.3 %reduce-scatter.8.cloned.1.call-done = f32[96,1024]{1,0:T(8,128)} async-done(((f32[1536,1024]{1,0:T(8,128)}), f32[96,1024]{1,0:T(8,128)}) %reduce-scatter.8.cloned.1.call-update) | async-done | bytes 393232
  433.7 0.0 copy-done.1
  (11 shorter events, 0.1 us)
Async XLA Ops:
  7.2 7.5 %copy-start = (bf16[1536,1024]{1,0:T(8,128)(2,1)S(1)}, bf16[1536,1024]{1,0:T(8,128)(2,1)}, u32[]{:S(2)}) copy-start(bf16[1536,1024]{1,0:T(8,128)(2,1)} %param.13) | copy-start | bytes 9437188
  11.0 3.7 copy-start.8
  19.9 8.2 %copy-start.5 = (bf16[1024]{0:T(1024)(128)(2,1)S(1)}, bf16[1024]{0:T(1024)(128)(2,1)}, u32[]{:S(2)}) copy-start(bf16[1024]{0:T(1024)(128)(2,1)} %param.14) | copy-start | bytes 6148
  19.9 39.8 %all-to-all-start = ((bf16[16,64,1024]{2,1,0:T(8,128)(2,1)}), bf16[16,64,1024]{2,1,0:T(8,128)(2,1)S(1)}, u32[]{:S(2)}, u32[]{:S(2)}) async-start(bf16[16,64,1024]{2,1,0:T(8,128)(2,1)} %copy.55), calls=%async_computation | async-start | bytes 4194304 | tf_op jit(solution)/shard_map/all_to_all | solution.py:77
  28.0 231.8 %all-reduce.4.cloned.1.call-start = ((), (), s32[]{:S(2)}) async-start(), calls=%async_computation.6 | async-start | bytes 9437184
  149.0 3.0 copy-start.3
  155.8 0.7 copy-start.6
  155.8 0.7 copy-start.7
  155.8 0.9 copy-start.4
  155.8 1.8 copy-start.2
  155.8 192.5 %reduce-scatter.6.cloned.1.call-start = ((), (), s32[]{:S(2)}) async-start(), calls=%async_computation.4 | async-start | bytes 8912896 | tf_op jit(solution)/shard_map/reduce_scatter | solution.py:127
  166.8 1.4 copy-start.9
  166.8 266.9 %reduce-scatter.8.cloned.1.call-start = ((), (), s32[]{:S(2)}) async-start(), calls=%async_computation.5 | async-start | bytes 6684672
  179.3 254.4 %copy-start.1 = (bf16[1536,1024]{1,0:T(8,128)(2,1)S(1)}, bf16[1536,1024]{1,0:T(8,128)(2,1)}, u32[]{:S(2)}) copy-start(bf16[1536,1024]{1,0:T(8,128)(2,1)} %param.13) | copy-start | bytes 9437188
  179.3 0.8 copy-start.10
Sparse Core Ops, SparseCore 0:
  156.0 103.8 all-reduce.3
  263.6 84.7 reduce-scatter.5
  352.8 80.9 reduce-scatter.7
